TPU v7x, 32 devices: a whole 2x2x4 slice. The times are simulated.
32 devices in a mesh: users: 2 (over x), hist: 8 (over z, y), head: 2 (over core).
Axes of the slice: x: 2, y: 2, z: 4, core: 2. Of those that a mesh axis runs over, the one named last changes fastest.
Arguments:
- candidates: bfloat16 [2048, 512], P(('users', 'hist')), parts along dimension 0, may hold values from -6 to 6
- key_cache: bfloat16 [2, 32768, 512], P(None, ('users', 'hist'), 'head'), parts along dimension 1, may hold values from -6 to 6
- value_cache: bfloat16 [2, 32768, 512], P(None, ('users', 'hist'), 'head'), parts along dimension 1, may hold values from -6 to 6
- w_in: bfloat16 [2, 512, 4, 512], P(None, None, None, 'head'), may hold values from -0.25 to 0.25
- w_out: bfloat16 [2, 512, 512], P(None, 'head'), may hold values from -0.25 to 0.25
- rab_table: float32 [2, 32, 8], P(None, None, 'head'), may hold values from -4 to 4
- hist_len: int32 [16], P(('users', 'hist')), parts along dimension 0, may hold values from 1 to 2048, 8192 in all
- hist_bucket: int32 [32768], P(('users', 'hist')), parts along dimension 0, may hold values from 0 to 31
- visible: int32 [8, 128], P(None, ('users', 'hist')), parts along dimension 1, may hold values 0 or 1
Outputs:
- candidate_out: bfloat16 [2048, 512], P(('users', 'hist')), parts along dimension 0
There are 2 independent parts, one for each index of `users`. A program takes and returns all parts, laid end to end along the dimension named above; an argument that names none is the same for every part. Nothing has to cross between parts.
Inputs may be any that keep to these rules, and one draw needn't show every extreme that they name: `hist_len`: entry s counts the valid events at the start of history shard s; the entries sum to 8192 and the largest is 2048. visible[m, b] is 1 where microbatch m sees history events b * 256 to (b + 1) * 256 - 1.
All inputs are finite; a program needn't handle non-finite values.
Results may differ from a plain program's by a relative error of at most 0.019.
Values may be sent and summed in bfloat16 or wider, within the bound.
A program may use at most 64 MiB of HBM per device.

v0:
```python
import jax
import jax.numpy as jnp
from jax import lax
from jax.sharding import PartitionSpec as P

D = 512
HEADS = 8
DH = 64
LAYERS = 2
NB = 32
BLOCK = 256
MICRO = 8
C = 1024


epsilon = 1e-05


def shards(
    candidates, key_cache, value_cache, w_in, w_out, rab_table, hist_len, hist_bucket, visible
):
    width = HEADS * DH
    factor = DH ** (-0.5)
    local_len = hist_len[0]
    hist_dev = key_cache.shape[1]
    width_local = key_cache.shape[2]
    heads_local = width_local // DH
    key_block = min(512, hist_dev)
    row_count = candidates.shape[0]
    visible_float = visible.astype(jnp.float32)
    stream = lax.all_gather(candidates, "hist", axis=0, tiled=True).astype(jnp.float32)
    for layer_index in range(LAYERS):
        project_average = jnp.mean(stream, axis=-1, keepdims=True)
        centred = stream - project_average
        variance = jnp.mean(centred * centred, axis=-1, keepdims=True)
        normed = (centred * lax.rsqrt(variance + epsilon)).astype(jnp.bfloat16)
        projected = jnp.dot(
            normed,
            w_in[layer_index].reshape(D, 4 * width_local),
            preferred_element_type=jnp.float32,
        )
        projected = jax.nn.silu(projected).astype(jnp.bfloat16).reshape(-1, 4, width_local)
        queries = projected[:, 0]
        keys_new = projected[:, 1]
        values_new = projected[:, 2]
        gates = projected[:, 3]
        one_hot = (hist_bucket[:, None] == jnp.arange(NB, dtype=jnp.int32)[None, :]).astype(
            jnp.float32
        )
        bias = jnp.dot(one_hot, rab_table[layer_index], precision=lax.Precision.HIGHEST)
        attend_query_count = queries.shape[0]
        micro_ids = jnp.arange(attend_query_count, dtype=jnp.int32) // (C // MICRO)
        picking = (micro_ids[:, None] == jnp.arange(MICRO, dtype=jnp.int32)[None, :]).astype(
            jnp.float32
        )
        visible_rows = jnp.dot(picking, visible_float, precision=lax.Precision.HIGHEST)
        attend_query_heads = queries.reshape(attend_query_count, heads_local, DH)
        cached_keys = key_cache[layer_index]
        cached_values = value_cache[layer_index]

        def block_step(block_index, summed):
            key_start = block_index * key_block

            def compute(held):
                key_part = lax.dynamic_slice_in_dim(cached_keys, key_start, key_block, 0).reshape(
                    key_block, heads_local, DH
                )
                value_part = lax.dynamic_slice_in_dim(
                    cached_values, key_start, key_block, 0
                ).reshape(key_block, heads_local, DH)
                bias_part = lax.dynamic_slice_in_dim(bias, key_start, key_block, 0)
                visible_part = lax.dynamic_slice_in_dim(
                    visible_rows, key_start // BLOCK, key_block // BLOCK, 1
                )
                positions = key_start + jnp.arange(key_block, dtype=jnp.int32)
                valid = (positions < local_len).astype(jnp.float32)
                masking = (
                    jnp.repeat(visible_part, BLOCK, axis=1, total_repeat_length=key_block)
                    * valid[None, :]
                )
                scores = jnp.einsum(
                    "rhd,khd->hrk", attend_query_heads, key_part, preferred_element_type=jnp.float32
                )
                scores = scores * factor + bias_part.T[:, None, :]
                weights = (jax.nn.silu(scores) * masking[None]).astype(jnp.bfloat16)
                return held + jnp.einsum(
                    "hrk,khd->rhd", weights, value_part, preferred_element_type=jnp.float32
                )

            return lax.cond(key_start < local_len, compute, lambda held: held, summed)

        summed = lax.fori_loop(
            0,
            hist_dev // key_block,
            block_step,
            jnp.zeros((attend_query_count, heads_local, DH), jnp.float32),
        )
        terms = summed.reshape(attend_query_count, width_local)
        attended = lax.psum(terms.astype(jnp.bfloat16), "hist").astype(jnp.float32)
        finish_attended = attended
        query_count = finish_attended.shape[0]
        query_heads = queries.astype(jnp.float32).reshape(query_count, heads_local, DH)
        key_heads = keys_new.astype(jnp.float32).reshape(query_count, heads_local, DH)
        value_heads = values_new.astype(jnp.float32).reshape(query_count, heads_local, DH)
        own_score = jax.nn.silu(jnp.sum(query_heads * key_heads, axis=-1) * factor)
        finish_attended = finish_attended + (own_score[..., None] * value_heads).reshape(
            query_count, width_local
        )
        totals = lax.psum(
            (
                jnp.sum(finish_attended, axis=-1),
                jnp.sum(finish_attended * finish_attended, axis=-1),
            ),
            "head",
        )
        average = (totals[0] / width)[:, None]
        squares = (totals[1] / width)[:, None]
        normalized = (finish_attended - average) * lax.rsqrt(squares - average * average + epsilon)
        gated = (normalized * gates.astype(jnp.float32)).astype(jnp.bfloat16)
        update = lax.psum(
            jnp.dot(gated, w_out[layer_index], preferred_element_type=jnp.float32).astype(
                jnp.bfloat16
            ),
            "head",
        ).astype(jnp.float32)
        stream = stream + update
    own_start = lax.axis_index("hist") * row_count
    return lax.dynamic_slice_in_dim(stream, own_start, row_count, 0).astype(jnp.bfloat16)


def solution(mesh):
    placed = (
        P(("users", "hist"), None),
        P(None, ("users", "hist"), "head"),
        P(None, ("users", "hist"), "head"),
        P(None, None, None, "head"),
        P(None, "head", None),
        P(None, None, "head"),
        P(("users", "hist")),
        P(("users", "hist")),
        P(None, ("users", "hist")),
    )
    return jax.shard_map(
        shards, mesh=mesh, in_specs=placed, out_specs=P(("users", "hist"), None), check_vma=False
    )
```

profile of v0, /device:TPU:1, one launch (start us, length us, event | category | flops | bytes accessed | tf_op | source)
XLA Modules:
  0.0 378.3 jit_solution(7019134319419471442)
XLA Ops:
  7.3 3.3 fusion.74
  19.4 30.8 %all-gather.2.cloned.1.call-done = bf16[1024,512]{1,0:T(8,128)(2,1)} async-done(((bf16[128,512]{1,0:T(8,128)(2,1)}), bf16[1024,512]{1,0:T(8,128)(2,1)}) %all-gather.2.cloned.1.call-update) | async-done | bytes 1048592 | tf_op jit(solution)/shard_map/all_gather | solution.py:31
  53.5 2.6 multiply_convert_fusion.1
  59.6 39.9 %while.34 = (s32[]{:T(128)}, f32[1024,4,64]{0,2,1:T(8,128)}, s32[]{:T(128)}, bf16[2048,256]{0,1:T(8,128)(2,1)}, bf16[2048,256]{0,1:T(8,128)(2,1)}, /*index=5*/bf...) while((s32[]{:T(128)}, f32[1024,4,64]{0,2,1:T(8,128)}, ...), condition=%wide.region_5.7_spmd, body=%wide.region_2.6_spmd.sunk | while | flops 554437120 | bytes 14733740 | solution.py:92
  60.3 12.4 %conditional.4 = (f32[1024,4,64]{0,2,1:T(8,128)}) conditional(s32[]{:T(128)} %convert_element_type.273, f32[1024,4,64]{0,2,1:T(8,128)} %get-tuple-element.543, (s32[]{:T(128)}, bf16[2048,256]{0,1:T(8,128)(2,1)}, bf16[2048,256]{0,1:T(8,128)(2,1)}, bf16[1024,4,64]{0,2,1:T(8,128)(2,1)}, f32[2048,4]{0,1:T(4,128)S(1)}, /*index=5*/f32[1024,8]{0,1:T(8,128)S(1)}, ...), branch_computations={%region_3.3_spmd, %region_4.5_spmd} | conditional | flops 554437120 | bytes 14733549 | solution.py:90
  61.0 1.8 gather_fusion
  66.1 6.6 %fusion.12 = f32[1024,4,64]{0,2,1:T(8,128)} fusion(f32[1024,4,64]{0,2,1:T(8,128)} %get-tuple-element.336, bf16[512,4,64]{0,2,1:T(8,128)(2,1)S(1)} %bitcast.148, f32[1024,512]{0,1:T(8,128)} %bitcast_multiply_fusion.1, f32[4,512]{1,0:T(4,128)S(1)} %dynamic-slice_bitcast_fusion, bf16[512,4,64]{0,2,1:T(8,128)(2,1)S(1)} %bitcast.147, ...), kind=kOutput, calls=%fused_computation.13 | convolution fusion | flops 553910272 | bytes 5251072 | tf_op jit(solution)/shard_map/while/body/eval_jaxpr/cond/branch_1_fun/hrk,khd->rhd/dot_general | solution.py:86
  73.3 12.4 %conditional.4 = (f32[1024,4,64]{0,2,1:T(8,128)}) conditional(s32[]{:T(128)} %convert_element_type.273, f32[1024,4,64]{0,2,1:T(8,128)} %get-tuple-element.543, (s32[]{:T(128)}, bf16[2048,256]{0,1:T(8,128)(2,1)}, bf16[2048,256]{0,1:T(8,128)(2,1)}, bf16[1024,4,64]{0,2,1:T(8,128)(2,1)}, f32[2048,4]{0,1:T(4,128)S(1)}, /*index=5*/f32[1024,8]{0,1:T(8,128)S(1)}, ...), branch_computations={%region_3.3_spmd, %region_4.5_spmd} | conditional | flops 554437120 | bytes 14733549 | solution.py:90
  74.1 1.8 gather_fusion
  79.2 6.6 %fusion.12 = f32[1024,4,64]{0,2,1:T(8,128)} fusion(f32[1024,4,64]{0,2,1:T(8,128)} %get-tuple-element.336, bf16[512,4,64]{0,2,1:T(8,128)(2,1)S(1)} %bitcast.148, f32[1024,512]{0,1:T(8,128)} %bitcast_multiply_fusion.1, f32[4,512]{1,0:T(4,128)S(1)} %dynamic-slice_bitcast_fusion, bf16[512,4,64]{0,2,1:T(8,128)(2,1)S(1)} %bitcast.147, ...), kind=kOutput, calls=%fused_computation.13 | convolution fusion | flops 553910272 | bytes 5251072 | tf_op jit(solution)/shard_map/while/body/eval_jaxpr/cond/branch_1_fun/hrk,khd->rhd/dot_general | solution.py:86
  86.4 12.4 %conditional.4 = (f32[1024,4,64]{0,2,1:T(8,128)}) conditional(s32[]{:T(128)} %convert_element_type.273, f32[1024,4,64]{0,2,1:T(8,128)} %get-tuple-element.543, (s32[]{:T(128)}, bf16[2048,256]{0,1:T(8,128)(2,1)}, bf16[2048,256]{0,1:T(8,128)(2,1)}, bf16[1024,4,64]{0,2,1:T(8,128)(2,1)}, f32[2048,4]{0,1:T(4,128)S(1)}, /*index=5*/f32[1024,8]{0,1:T(8,128)S(1)}, ...), branch_computations={%region_3.3_spmd, %region_4.5_spmd} | conditional | flops 554437120 | bytes 14733549 | solution.py:90
  87.2 1.8 gather_fusion
  92.3 6.6 %fusion.12 = f32[1024,4,64]{0,2,1:T(8,128)} fusion(f32[1024,4,64]{0,2,1:T(8,128)} %get-tuple-element.336, bf16[512,4,64]{0,2,1:T(8,128)(2,1)S(1)} %bitcast.148, f32[1024,512]{0,1:T(8,128)} %bitcast_multiply_fusion.1, f32[4,512]{1,0:T(4,128)S(1)} %dynamic-slice_bitcast_fusion, bf16[512,4,64]{0,2,1:T(8,128)(2,1)S(1)} %bitcast.147, ...), kind=kOutput, calls=%fused_computation.13 | convolution fusion | flops 553910272 | bytes 5251072 | tf_op jit(solution)/shard_map/while/body/eval_jaxpr/cond/branch_1_fun/hrk,khd->rhd/dot_general | solution.py:86
  99.5 2.2 convert_element_type.165
  102.1 83.6 %all-reduce.7.cloned.1.call-done = bf16[1024,256]{0,1:T(8,128)(2,1)} async-done(((bf16[1024,256]{0,1:T(8,128)(2,1)}), bf16[1024,256]{0,1:T(8,128)(2,1)}) %all-reduce.7.cloned.1.call-update) | async-done | bytes 524304 | tf_op jit(solution)/shard_map/psum | solution.py:99
  187.1 4.5 %all-reduce.1 = (f32[1024]{0:T(1024)S(1)}, f32[1024]{0:T(1024)S(1)}) all-reduce(f32[1024]{0:T(1024)S(1)} %get-tuple-element.377, f32[1024]{0:T(1024)S(1)} %get-tuple-element.376), channel_id=1, replica_groups=mesh['users'=2,'hist'=8,'head'=2] {'head'}, use_global_device_ids=true, to_apply=%region_11.13 | all-reduce | flops 2048 | bytes 16384 | tf_op jit(solution)/shard_map/psum | solution.py:109
  193.4 2.5 convolution_convert_fusion.1
  201.1 13.8 %all-reduce.9.cloned.1.call-done = bf16[1024,512]{1,0:T(8,128)(2,1)} async-done(((bf16[1024,512]{1,0:T(8,128)(2,1)}), bf16[1024,512]{1,0:T(8,128)(2,1)}) %all-reduce.9.cloned.1.call-update) | async-done | bytes 1048592 | tf_op jit(solution)/shard_map/psum | solution.py:120
  218.4 2.7 multiply_convert_fusion
  222.9 36.5 %while.35 = (s32[]{:T(128)}, f32[1024,4,64]{0,2,1:T(8,128)S(1)}, s32[]{:T(128)}, bf16[2048,256]{0,1:T(8,128)(2,1)}, bf16[2048,256]{0,1:T(8,128)(2,1)}, /*index=5...) while((s32[]{:T(128)}, f32[1024,4,64]{0,2,1:T(8,128)S(1)}, ...), condition=%wide.region_18.20_spmd, body=%wide.region_15.19_spmd.sunk | while | flops 554437120 | bytes 14733740 | solution.py:92
  223.5 11.3 %conditional.5 = (f32[1024,4,64]{0,2,1:T(8,128)S(1)}) conditional(s32[]{:T(128)} %convert_element_type.274, f32[1024,4,64]{0,2,1:T(8,128)S(1)} %get-tuple-element.573, (s32[]{:T(128)}, bf16[2048,256]{0,1:T(8,128)(2,1)}, bf16[2048,256]{0,1:T(8,128)(2,1)}, bf16[1024,4,64]{0,2,1:T(8,128)(2,1)}, f32[2048,4]{0,1:T(4,128)S(1)}, ...), branch_computations={%region_16.17_spmd, %region_17.18_spmd} | conditional | flops 554437120 | bytes 14733549 | solution.py:90
  224.3 1.8 gather_fusion.1
  229.4 5.4 %fusion.30 = f32[1024,4,64]{0,2,1:T(8,128)S(1)} fusion(f32[1024,4,64]{0,2,1:T(8,128)S(1)} %get-tuple-element.353, bf16[512,4,64]{0,2,1:T(8,128)(2,1)S(1)} %bitcast.150, f32[1024,512]{0,1:T(8,128)} %bitcast_multiply_fusion.3, f32[4,512]{1,0:T(4,128)S(1)} %dynamic-slice_bitcast_fusion.1, bf16[512,4,64]{0,2,1:T(8,128)(2,1)S(1)} %bitcast.149, ...), kind=kOutput, calls=%fused_computation.34 | convolution fusion | flops 553910272 | bytes 5251072 | tf_op jit(solution)/shard_map/while/body/eval_jaxpr/cond/branch_1_fun/hrk,khd->rhd/dot_general | solution.py:86
  235.5 11.3 %conditional.5 = (f32[1024,4,64]{0,2,1:T(8,128)S(1)}) conditional(s32[]{:T(128)} %convert_element_type.274, f32[1024,4,64]{0,2,1:T(8,128)S(1)} %get-tuple-element.573, (s32[]{:T(128)}, bf16[2048,256]{0,1:T(8,128)(2,1)}, bf16[2048,256]{0,1:T(8,128)(2,1)}, bf16[1024,4,64]{0,2,1:T(8,128)(2,1)}, f32[2048,4]{0,1:T(4,128)S(1)}, ...), branch_computations={%region_16.17_spmd, %region_17.18_spmd} | conditional | flops 554437120 | bytes 14733549 | solution.py:90
  236.2 1.8 gather_fusion.1
  241.4 5.4 %fusion.30 = f32[1024,4,64]{0,2,1:T(8,128)S(1)} fusion(f32[1024,4,64]{0,2,1:T(8,128)S(1)} %get-tuple-element.353, bf16[512,4,64]{0,2,1:T(8,128)(2,1)S(1)} %bitcast.150, f32[1024,512]{0,1:T(8,128)} %bitcast_multiply_fusion.3, f32[4,512]{1,0:T(4,128)S(1)} %dynamic-slice_bitcast_fusion.1, bf16[512,4,64]{0,2,1:T(8,128)(2,1)S(1)} %bitcast.149, ...), kind=kOutput, calls=%fused_computation.34 | convolution fusion | flops 553910272 | bytes 5251072 | tf_op jit(solution)/shard_map/while/body/eval_jaxpr/cond/branch_1_fun/hrk,khd->rhd/dot_general | solution.py:86
  247.4 11.3 %conditional.5 = (f32[1024,4,64]{0,2,1:T(8,128)S(1)}) conditional(s32[]{:T(128)} %convert_element_type.274, f32[1024,4,64]{0,2,1:T(8,128)S(1)} %get-tuple-element.573, (s32[]{:T(128)}, bf16[2048,256]{0,1:T(8,128)(2,1)}, bf16[2048,256]{0,1:T(8,128)(2,1)}, bf16[1024,4,64]{0,2,1:T(8,128)(2,1)}, f32[2048,4]{0,1:T(4,128)S(1)}, ...), branch_computations={%region_16.17_spmd, %region_17.18_spmd} | conditional | flops 554437120 | bytes 14733549 | solution.py:90
  248.2 1.8 gather_fusion.1
  253.3 5.4 %fusion.30 = f32[1024,4,64]{0,2,1:T(8,128)S(1)} fusion(f32[1024,4,64]{0,2,1:T(8,128)S(1)} %get-tuple-element.353, bf16[512,4,64]{0,2,1:T(8,128)(2,1)S(1)} %bitcast.150, f32[1024,512]{0,1:T(8,128)} %bitcast_multiply_fusion.3, f32[4,512]{1,0:T(4,128)S(1)} %dynamic-slice_bitcast_fusion.1, bf16[512,4,64]{0,2,1:T(8,128)(2,1)S(1)} %bitcast.149, ...), kind=kOutput, calls=%fused_computation.34 | convolution fusion | flops 553910272 | bytes 5251072 | tf_op jit(solution)/shard_map/while/body/eval_jaxpr/cond/branch_1_fun/hrk,khd->rhd/dot_general | solution.py:86
  261.9 80.7 %all-reduce.11.cloned.1.call-done = bf16[1024,256]{0,1:T(8,128)(2,1)} async-done(((bf16[1024,256]{0,1:T(8,128)(2,1)}), bf16[1024,256]{0,1:T(8,128)(2,1)}) %all-reduce.11.cloned.1.call-update) | async-done | bytes 524304 | tf_op jit(solution)/shard_map/psum | solution.py:99
  343.9 4.5 %all-reduce = (f32[1024]{0:T(1024)S(1)}, f32[1024]{0:T(1024)S(1)}) all-reduce(f32[1024]{0:T(1024)S(1)} %get-tuple-element.375, f32[1024]{0:T(1024)S(1)} %get-tuple-element.374), channel_id=1, replica_groups=mesh['users'=2,'hist'=8,'head'=2] {'head'}, use_global_device_ids=true, to_apply=%region_24.26 | all-reduce | flops 2048 | bytes 16384 | tf_op jit(solution)/shard_map/psum | solution.py:109
  351.3 18.8 %all-reduce.13.cloned.1.call-done = bf16[1024,512]{1,0:T(8,128)(2,1)} async-done(((bf16[1024,512]{1,0:T(8,128)(2,1)}), bf16[1024,512]{1,0:T(8,128)(2,1)}) %all-reduce.13.cloned.1.call-update) | async-done | bytes 1048592 | tf_op jit(solution)/shard_map/psum | solution.py:120
  (121 shorter events, 62.1 us)
Async XLA Ops:
  6.5 43.7 %all-gather.2.cloned.1.call-start = ((), (), s32[]{:S(2)}) async-start(), calls=%async_computation | async-start | bytes 1179648 | tf_op jit(solution)/shard_map/all_gather | solution.py:31
  7.3 178.4 %all-reduce.7.cloned.1.call-start = ((), (), s32[]{:S(2)}) async-start(), calls=%async_computation.1 | async-start | bytes 1048576 | tf_op jit(solution)/shard_map/psum | solution.py:99
  10.6 2.0 copy-start.8
  13.6 2.0 copy-start.9
  16.7 1.5 copy-start.16
  16.8 1.9 copy-start.15
  16.8 2.0 copy-start.17
  16.8 36.7 %copy-start.12 = (bf16[64,8,4,256]{3,1,2,0:T(8,128)(2,1)S(1)}, bf16[64,8,4,256]{3,1,2,0:T(8,128)(2,1)}, u32[]{:S(2)}) copy-start(bf16[64,8,4,256]{3,1,2,0:T(8,128)(2,1)} %copy.22) | copy-start | bytes 3145732
  50.2 3.3 copy-start
  56.1 1.3 copy-start.7
  99.5 2.3 copy-start.10
  99.5 2.3 copy-start.11
  101.8 113.1 %all-reduce.9.cloned.1.call-start = ((), (), s32[]{:S(2)}) async-start(), calls=%async_computation.2 | async-start | bytes 2097152 | tf_op jit(solution)/shard_map/psum | solution.py:120
  191.7 4.6 %copy-start.1 = (bf16[1,512,4,256]{3,2,1,0:T(4,128)(2,1)S(1)}, bf16[1,512,4,256]{3,2,1,0:T(4,128)(2,1)}, u32[]{:S(2)}) copy-start(bf16[1,512,4,256]{3,2,1,0:T(4,128)(2,1)} %get-tuple-element.422) | copy-start | bytes 3145732
  193.4 4.0 %copy-start.2 = (bf16[1,2048,256]{2,1,0:T(8,128)(2,1)S(1)}, bf16[1,2048,256]{2,1,0:T(8,128)(2,1)}, u32[]{:S(2)}) copy-start(bf16[1,2048,256]{2,1,0:T(8,128)(2,1)} %get-tuple-element.426) | copy-start | bytes 3145732
  196.0 146.6 %all-reduce.11.cloned.1.call-start = ((), (), s32[]{:S(2)}) async-start(), calls=%async_computation.3 | async-start | bytes 1048576 | tf_op jit(solution)/shard_map/psum | solution.py:99
  197.5 1.4 copy-start.3
  214.8 1.7 copy-start.4
  216.5 1.9 copy-start.13
  221.0 1.7 copy-start.5
  259.4 83.2 %copy-start.6 = (bf16[1024,1024]{0,1:T(8,128)(2,1)S(1)}, bf16[1024,1024]{0,1:T(8,128)(2,1)}, u32[]{:S(2)}) copy-start(bf16[1024,1024]{0,1:T(8,128)(2,1)} %copy-done.5) | copy-start | bytes 6291460
  260.3 109.8 %all-reduce.13.cloned.1.call-start = ((), (), s32[]{:S(2)}) async-start(), calls=%async_computation.4 | async-start | bytes 2097152 | tf_op jit(solution)/shard_map/psum | solution.py:120
  260.4 89.4 %copy-start.14 = (bf16[2,256,512]{2,1,0:T(8,128)(2,1)S(1)}, bf16[2,256,512]{2,1,0:T(8,128)(2,1)}, u32[]{:S(2)}) copy-start(bf16[2,256,512]{2,1,0:T(8,128)(2,1)} %param.27) | copy-start | bytes 1572868
Sparse Core Ops, SparseCore 0:
  9.5 40.7 all-gather.1
  101.9 83.7 all-reduce.6
  196.1 18.6 all-reduce.8
  260.4 82.0 all-reduce.10
  351.4 18.6 all-reduce.12
where the time goes:
time: 380 us; the launch traced here: 378 us
  waiting for transfers between devices  228 us (60%)
  matrix products  47.1 us (12%)
  local copies, waits for them, and re-layouts  37.9 us (10%)
  other arithmetic  36.2 us (10%)
  between operations  13.4 us (4%)
  blocking collectives  9.09 us (2%)
  loops' own time  5.82 us (2%)
    psum x2, waiting for transfers between devices, shards(): attended = lax.psum(terms.astype(jnp.bfloat16), 'hist').astype(jnp.float32)  164 us
    dot_general x6, matrix products, compute(): jnp.einsum('hrk,khd->rhd', weights, value_part, preferred_element_type=jn...  35.9 us
    psum x2, waiting for transfers between devices, shards(): lax.psum(jnp.dot(gated, w_out[layer_index], preferred_element_type=jnp.fl...  32.6 us
    all_gather x1, waiting for transfers between devices, shards(): lax.all_gather(candidates, 'hist', axis=0, tiled=True).astype(jnp.float32)  30.8 us
    unnamed x42, local copies, waits for them, and re-layouts  11.4 us
    gather x6, local copies, waits for them, and re-layouts, compute(): jnp.repeat(visible_part, BLOCK, axis=1, total_repeat_length=key_block)  11 us
    psum x2, blocking collectives, shards(): lax.psum((jnp.sum(finish_attended, axis=-1), jnp.sum(finish_attended * fi...  9.09 us
    mul x6, other arithmetic, compute(): jnp.repeat(visible_part, BLOCK, axis=1, total_repeat_length=key_block)  9.09 us
  transfers between devices with their start and end apart: 5, of which 5 were waited for; matrix products, arithmetic and copies ran while one was open for 5% of the time, Pallas kernels for 0%

commit v1 on v0

v1 whole, which is shorter than its diff:
```python
import functools

import jax
import jax.numpy as jnp
from jax import lax
from jax.experimental import pallas as pl
from jax.experimental.pallas import tpu as pltpu
from jax.sharding import PartitionSpec as P

DH = 64
BLOCK = 256
LANES = 128
PER = LANES // DH
GROUP_ROWS = 256
KEY_CHUNK = 512
BIG = 16384.0
MESH = pl.DeviceIdType.MESH

epsilon = 1e-05


def silu(v):
    return v / (1.0 + jnp.exp(-v))


def dot(a, b):
    return jnp.dot(a, b, preferred_element_type=jnp.float32)


def kernel(
    n,
    cand,
    w_in,
    key_hbm,
    val_hbm,
    w_out,
    rab,
    bucket,
    hlen,
    vis,
    out,
    keys,
    vals,
    kaug,
    table,
    events,
    w_other,
    qall,
    qaug,
    part,
    parts_in,
    acc,
    att_send,
    att_in,
    gate_send,
    gate_in,
    load_sem,
    q_send,
    q_recv,
    p_send,
    p_recv,
    h_send,
    h_recv,
):
    me = lax.axis_index("hist")
    other = 1 - lax.axis_index("head")
    layers, hist_dev, wl = key_hbm.shape
    rows, d = cand.shape
    heads = wl // DH
    pairs = wl // LANES
    nb = rab.shape[1]
    micro, blocks = vis.shape
    total = n * rows
    micro_rows = total // micro
    group_rows = min(GROUP_ROWS, total)
    per_group = group_rows // rows
    groups = n // per_group
    key_chunk = min(KEY_CHUNK, hist_dev)

    load_k = pltpu.make_async_copy(key_hbm, keys, load_sem.at[0])
    load_v = pltpu.make_async_copy(val_hbm, vals, load_sem.at[1])
    load_k.start()
    load_v.start()

    barrier = pltpu.get_barrier_semaphore()
    for j in range(1, n):
        pl.semaphore_signal(
            barrier, inc=1, device_id={"hist": lax.rem(me + j, n)}, device_id_type=MESH
        )
    pl.semaphore_signal(barrier, inc=1, device_id={"head": other}, device_id_type=MESH)

    def to_head(src, dst, index):
        return pltpu.make_async_remote_copy(
            src_ref=src,
            dst_ref=dst,
            send_sem=h_send.at[index],
            recv_sem=h_recv.at[index],
            device_id={"head": other},
            device_id_type=MESH,
        )

    def row_of(s):
        return pl.ds(pl.multiple_of(s * rows, rows), rows)

    def q_copy(l, s, owner):
        return pltpu.make_async_remote_copy(
            src_ref=qall.at[l, row_of(owner)],
            dst_ref=qall.at[l, row_of(owner)],
            send_sem=q_send.at[l, s],
            recv_sem=q_recv.at[l, owner],
            device_id={"hist": s},
            device_id_type=MESH,
        )

    def p_copy(l, s, owner):
        return pltpu.make_async_remote_copy(
            src_ref=part.at[l, row_of(s)],
            dst_ref=parts_in.at[l, owner],
            send_sem=p_send.at[l, s],
            recv_sem=p_recv.at[l, owner],
            device_id={"hist": s},
            device_id_type=MESH,
        )

    def build_keys():
        lane = lax.broadcasted_iota(jnp.int32, (LANES, LANES), 1)
        lane8 = lax.broadcasted_iota(jnp.int32, (blocks, LANES), 1)
        row8 = lax.broadcasted_iota(jnp.int32, (blocks, LANES), 0)
        base_of = (DH, 0)
        seen = []
        gone = []
        for base in base_of:
            held = jnp.zeros((blocks, LANES), jnp.float32)
            for m in range(micro):
                column = jnp.zeros((blocks, LANES), jnp.float32)
                for b in range(blocks):
                    value = (vis[m, b] - 1).astype(jnp.float32) * BIG
                    column = jnp.where(row8 == b, value, column)
                held = jnp.where(lane8 == base + 2 + m, column, held)
            seen.append(held)
            is_micro = (lane8 >= base + 2) & (lane8 < base + 2 + micro)
            gone.append(jnp.where(is_micro & (row8 == 0), -BIG, 0.0))
        for l in range(layers):
            for h in range(heads):
                base = base_of[h % PER]
                half = rab[l][:, h : h + 1] * 0.5
                high = half.astype(jnp.bfloat16).astype(jnp.float32)
                low = half - high
                lane_nb = lane[:nb]
                bias = jnp.where(lane_nb == base, high, jnp.where(lane_nb == base + 1, low, 0.0))
                fill = jnp.zeros((LANES - nb - 2 * blocks, LANES), jnp.float32)
                whole = jnp.concatenate([bias, seen[h % PER], gone[h % PER], fill], axis=0)
                start = (l * heads + h) * LANES
                table[:, start : start + LANES] = whole.astype(jnp.bfloat16)

        row = lax.broadcasted_iota(jnp.int32, (LANES, key_chunk), 0)
        spot = lax.broadcasted_iota(jnp.int32, (LANES, key_chunk), 1)
        lane_k = lax.broadcasted_iota(jnp.int32, (key_chunk, LANES), 1)
        length = hlen[0]
        for c in range(hist_dev // key_chunk):
            span = slice(c * key_chunk, (c + 1) * key_chunk)
            place = spot + c * key_chunk
            here = (
                (row == bucket[:, span])
                | (row == nb + place // BLOCK)
                | ((row == nb + blocks) & (place >= length))
            )
            events[span, :] = jnp.where(here, 1.0, 0.0).T.astype(jnp.bfloat16)
        load_k.wait()

        def chunk(c, carry):
            span = pl.ds(pl.multiple_of(c * key_chunk, key_chunk), key_chunk)
            spread = events[span, :]
            for l in range(layers):
                for h in range(heads):
                    start = (l * heads + h) * LANES
                    extra = dot(spread, table[:, start : start + LANES])
                    p = h // PER
                    tile = keys[l, span, p * LANES : (p + 1) * LANES].astype(jnp.float32)
                    mine = (lane_k < DH) if h % PER == 0 else (lane_k >= DH)
                    kaug[l, h, span, :] = jnp.where(mine, tile, extra).astype(jnp.bfloat16)
            return carry

        lax.fori_loop(0, hist_dev // key_chunk, chunk, 0)

    lane_q = lax.broadcasted_iota(jnp.int32, (group_rows, LANES), 1)
    row_q = lax.broadcasted_iota(jnp.int32, (group_rows, LANES), 0)
    lane_a = lax.broadcasted_iota(jnp.int32, (group_rows, LANES), 1)

    def attend(l, g):
        span = pl.ds(pl.multiple_of(g * group_rows, group_rows), group_rows)
        which = (row_q + g * group_rows) // micro_rows
        for h in range(heads):
            p = h // PER
            base = DH if h % PER == 0 else 0
            tile = qall[l, span, p * LANES : (p + 1) * LANES].astype(jnp.float32)
            ones = (lane_q == base) | (lane_q == base + 1) | (lane_q == base + 2 + which)
            mine = (lane_q < DH) if h % PER == 0 else (lane_q >= DH)
            qaug[h] = jnp.where(mine, tile, jnp.where(ones, 1.0, 0.0)).astype(jnp.bfloat16)
        acc[...] = jnp.zeros_like(acc)

        def chunk(c, carry):
            keys_at = pl.ds(pl.multiple_of(c * key_chunk, key_chunk), key_chunk)
            for p in range(pairs):
                value = vals[l, keys_at, p * LANES : (p + 1) * LANES]
                found = []
                for e in range(PER):
                    h = p * PER + e
                    y = lax.dot_general(
                        qaug[h],
                        kaug[l, h, keys_at, :],
                        (((1,), (1,)), ((), ())),
                        preferred_element_type=jnp.float32,
                    ).astype(jnp.bfloat16)
                    weight = y * (jnp.tanh(y) + 1.0)
                    found.append(dot(weight, value))
                acc[:, p * LANES : (p + 1) * LANES] += jnp.where(lane_a < DH, found[0], found[1])
            return carry

        lax.fori_loop(0, hist_dev // key_chunk, chunk, 0)
        part[l, span, :] = acc[...].astype(jnp.bfloat16)

    block_row = lax.broadcasted_iota(jnp.int32, (wl, wl), 0) // DH
    block_col = lax.broadcasted_iota(jnp.int32, (wl, wl), 1) // DH
    same_head = jnp.where(block_row == block_col, 1.0, 0.0).astype(jnp.bfloat16)

    stream = cand[...].astype(jnp.float32)
    for l in range(layers):
        average = jnp.mean(stream, axis=-1, keepdims=True)
        centred = stream - average
        variance = jnp.mean(centred * centred, axis=-1, keepdims=True)
        normed = (centred * lax.rsqrt(variance + epsilon)).astype(jnp.bfloat16)

        def project(i):
            return silu(dot(normed, w_in[l, :, i * wl : (i + 1) * wl])).astype(jnp.bfloat16)

        queries = project(0).astype(jnp.float32)
        qall[l, row_of(me), :] = (queries * (0.5 * DH**-0.5)).astype(jnp.bfloat16)
        if l == 0:
            pl.semaphore_wait(barrier, n)
        for j in range(1, n):
            q_copy(l, lax.rem(me + j, n), me).start()
        keys_new = project(1).astype(jnp.float32)
        values_new = project(2).astype(jnp.float32)
        gates = project(3)
        gate_send[l] = gates
        gate_copy = to_head(gate_send.at[l], gate_in.at[l], 2 * l)
        gate_copy.start()
        if l == 0:
            w_copy = to_head(w_out, w_other, 2 * layers)
            w_copy.start()
        product = queries * keys_new
        high = product.astype(jnp.bfloat16)
        low = (product - high.astype(jnp.float32)).astype(jnp.bfloat16)
        own_score = dot(high, same_head) + dot(low, same_head)
        own = silu(own_score * (DH**-0.5)) * values_new
        if l == 0:
            build_keys()
            load_v.wait()

        def group(t, carry):
            g = lax.rem(me // per_group + t, groups)
            for i in range(per_group):
                s = g * per_group + i

                @pl.when(s != me)
                def _():
                    q_copy(l, s, s).wait_recv()

            attend(l, g)
            for i in range(per_group):
                s = g * per_group + i

                @pl.when(s != me)
                def _():
                    p_copy(l, s, me).start()

            return carry

        lax.fori_loop(0, groups, group, 0)
        history = part[l, row_of(me), :].astype(jnp.float32)
        for j in range(1, n):
            s = lax.rem(me + j, n)
            p_copy(l, s, s).wait_recv()
            history = history + parts_in[l, s].astype(jnp.float32)
        attended = history + own
        att_send[l] = attended
        att_copy = to_head(att_send.at[l], att_in.at[l], 2 * l + 1)
        att_copy.start()
        if l == 0:
            w_copy.wait_recv()
        gate_copy.wait_recv()
        att_copy.wait_recv()
        theirs = att_in[l]
        width = 2 * wl
        mean = (
            jnp.sum(attended, axis=-1, keepdims=True) + jnp.sum(theirs, axis=-1, keepdims=True)
        ) / width
        square = (
            jnp.sum(attended * attended, axis=-1, keepdims=True)
            + jnp.sum(theirs * theirs, axis=-1, keepdims=True)
        ) / width
        rstd = lax.rsqrt(square - mean * mean + epsilon)
        gated = ((attended - mean) * rstd * gates.astype(jnp.float32)).astype(jnp.bfloat16)
        gated_other = ((theirs - mean) * rstd * gate_in[l].astype(jnp.float32)).astype(
            jnp.bfloat16
        )
        stream = stream + (dot(gated, w_out[l]) + dot(gated_other, w_other[l]))
        gate_copy.wait_send()
        att_copy.wait_send()
        if l == 0:
            w_copy.wait_send()
        for j in range(1, n):
            s = lax.rem(me + j, n)
            q_copy(l, s, me).wait_send()
            p_copy(l, s, me).wait_send()
    out[...] = stream.astype(out.dtype)


def shards(
    n, candidates, key_cache, value_cache, w_in, w_out, rab_table, hist_len, hist_bucket, visible
):
    layers, hist_dev, wl = key_cache.shape
    rows, d = candidates.shape
    heads = wl // DH
    total = n * rows
    group_rows = min(GROUP_ROWS, total)
    bf16, f32 = jnp.bfloat16, jnp.float32
    vmem = pl.BlockSpec(memory_space=pltpu.VMEM)
    smem = pl.BlockSpec(memory_space=pltpu.SMEM)
    hbm = pl.BlockSpec(memory_space=pl.ANY)
    dma = pltpu.SemaphoreType.DMA
    return pl.pallas_call(
        functools.partial(kernel, n),
        out_shape=jax.ShapeDtypeStruct((rows, d), bf16),
        in_specs=[vmem, vmem, hbm, hbm, vmem, vmem, vmem, smem, smem],
        out_specs=vmem,
        scratch_shapes=[
            pltpu.VMEM((layers, hist_dev, wl), bf16),
            pltpu.VMEM((layers, hist_dev, wl), bf16),
            pltpu.VMEM((layers, heads, hist_dev, LANES), bf16),
            pltpu.VMEM((LANES, layers * heads * LANES), bf16),
            pltpu.VMEM((hist_dev, LANES), bf16),
            pltpu.VMEM(w_out.shape, bf16),
            pltpu.VMEM((layers, total, wl), bf16),
            pltpu.VMEM((heads, group_rows, LANES), bf16),
            pltpu.VMEM((layers, total, wl), bf16),
            pltpu.VMEM((layers, n, rows, wl), bf16),
            pltpu.VMEM((group_rows, wl), f32),
            pltpu.VMEM((layers, rows, wl), f32),
            pltpu.VMEM((layers, rows, wl), f32),
            pltpu.VMEM((layers, rows, wl), bf16),
            pltpu.VMEM((layers, rows, wl), bf16),
            dma((2,)),
            dma((layers, n)),
            dma((layers, n)),
            dma((layers, n)),
            dma((layers, n)),
            dma((2 * layers + 1,)),
            dma((2 * layers + 1,)),
        ],
        compiler_params=pltpu.CompilerParams(
            collective_id=0, has_side_effects=True, vmem_limit_bytes=48 * 1024 * 1024
        ),
    )(
        candidates,
        w_in.reshape(layers, d, 4 * wl),
        key_cache,
        value_cache,
        w_out,
        rab_table,
        hist_bucket.reshape(1, hist_dev),
        hist_len,
        visible,
    )


def solution(mesh):
    placed = (
        P(("users", "hist"), None),
        P(None, ("users", "hist"), "head"),
        P(None, ("users", "hist"), "head"),
        P(None, None, None, "head"),
        P(None, "head", None),
        P(None, None, "head"),
        P(("users", "hist")),
        P(("users", "hist")),
        P(None, ("users", "hist")),
    )
    return jax.shard_map(
        functools.partial(shards, mesh.shape["hist"]),
        mesh=mesh,
        in_specs=placed,
        out_specs=P(("users", "hist"), None),
        check_vma=False,
    )
```

time: 380 us -> 78 us (0.21)
  waiting for transfers between devices: 228 us -> 0 us
  Pallas kernels: 0 us -> 70.7 us
  matrix products: 47.1 us -> 0 us
  other arithmetic: 36.2 us -> 0 us
  local copies, waits for them, and re-layouts: 37.9 us -> 6.34 us
  between operations: 13.4 us -> 0.73 us
  blocking collectives: 9.09 us -> 0 us
  loops' own time: 5.82 us -> 0 us
    psum x4 -> x0, waiting for transfers between devices: 197 us -> none  [the longest x2 164 us: shards(): attended = lax.psum(terms.astype(jnp.bfloat16), 'hist').astype(jnp.float32)]
    pallas_call x0 -> x1, Pallas kernels: none -> 70.7 us  [shards(): pl.pallas_call(functools.partial(kernel, n), out_shape=jax.ShapeDtypeStru...]
    dot_general x13 -> x0, matrix products: 47.1 us -> none  [the longest x6 35.9 us: compute(): jnp.einsum('hrk,khd->rhd', weights, value_part, preferred_element_type=jn...]
    all_gather x1 -> x0, waiting for transfers between devices: 30.8 us -> none  [shards(): lax.all_gather(candidates, 'hist', axis=0, tiled=True).astype(jnp.float32)]
    convert_element_type x11 -> x0, other arithmetic: 11.8 us -> none  [the longest x6 3.91 us: compute(): valid = (positions < local_len).astype(jnp.float32)]
    reduce_sum x8 -> x0, other arithmetic: 11.1 us -> none  [the longest x2 3.52 us: shards(): variance = jnp.mean(centred * centred, axis=-1, keepdims=True)]
    gather x6 -> x0, local copies, waits for them, and re-layouts: 11 us -> none  [compute(): jnp.repeat(visible_part, BLOCK, axis=1, total_repeat_length=key_block)]
    mul x8 -> x0, other arithmetic: 9.13 us -> none  [the longest x6 9.09 us: compute(): jnp.repeat(visible_part, BLOCK, axis=1, total_repeat_length=key_block)]
  transfers between devices with their start and end apart: 5 -> 0, of which waited for: 5 -> 0; matrix products, arithmetic and copies ran while one was open for 5% -> 0% of each run, Pallas kernels for 0% -> 0%
where the time goes in v1:
time: 78 us; the launch traced here: 77.8 us
  Pallas kernels  70.7 us (91%)
  local copies, waits for them, and re-layouts  6.34 us (8%)
    pallas_call x1, Pallas kernels, shards(): pl.pallas_call(functools.partial(kernel, n), out_shape=jax.ShapeDtypeStru...  70.7 us
    reshape x1, local copies, waits for them, and re-layouts, shards(): w_in.reshape(layers, d, 4 * wl)  3.29 us
    unnamed x12, local copies, waits for them, and re-layouts  3.04 us

profile of v1, /device:TPU:1, one launch (start us, length us, event | category | flops | bytes accessed | tf_op | source)
XLA Modules:
  0.0 77.8 jit_solution(1942449576270303955)
XLA Ops:
  0.7 0.8 copy.10.rab
  1.4 0.0 copy-start.1
  1.4 0.0 copy-start.2
  1.4 0.0 copy-start.3
  1.5 0.0 copy-start.4
  1.5 3.3 %reshape.6.w_in = bf16[2,512,1024]{2,1,0:T(8,128)(2,1)S(1)} reshape(bf16[2,512,4,256]{3,2,1,0:T(4,128)(2,1)} %param.12) | data formatting | bytes 4194304 | tf_op jit(solution)/shard_map/reshape | solution.py:367
  4.8 0.0 copy-done.1
  4.8 0.0 copy-done.2
  4.8 0.0 copy-done.3
  4.8 0.0 copy-done.4
  4.8 0.0 copy-start
  4.8 1.6 %copy-done = bf16[2,2048,256]{2,1,0:T(8,128)(2,1)S(1)} copy-done((bf16[2,2048,256]{2,1,0:T(8,128)(2,1)S(1)}, bf16[2,2048,256]{2,1,0:T(8,128)(2,1)}, u32[]{:S(2)}) %copy-start) | copy-done | bytes 2097176
  6.4 70.7 %shard_map.91 = bf16[128,512]{1,0:T(8,128)(2,1)S(1)} custom-call(bf16[128,512]{1,0:T(8,128)(2,1)S(1)} %copy-done.2, bf16[2,512,1024]{2,1,0:T(8,128)(2,1)S(1)} %reshape.6.w_in, bf16[2,2048,256]{2,1,0:T(8,128)(2,1)S(1)} %copy-done, bf16[2,2048,256]{2,1,0:T(8,128)(2,1)} %val_hbm.1, bf16[2,256,512]{2,1,0:T(8,128)(2,1)S(1)} %copy-done.1, ...), custom_call_target="tpu_custom_call" | custom-call | tf_op jit(solution)/shard_map/pallas_call | solution.py:333
  77.1 0.7 copy.13
Async XLA Ops:
  1.4 3.3 %copy-start.1 = (bf16[2,256,512]{2,1,0:T(8,128)(2,1)S(1)}, bf16[2,256,512]{2,1,0:T(8,128)(2,1)}, u32[]{:S(2)}) copy-start(bf16[2,256,512]{2,1,0:T(8,128)(2,1)} %w_out.1) | copy-start | bytes 1572868
  1.4 3.4 %copy-start.2 = (bf16[128,512]{1,0:T(8,128)(2,1)S(1)}, bf16[128,512]{1,0:T(8,128)(2,1)}, u32[]{:S(2)}) copy-start(bf16[128,512]{1,0:T(8,128)(2,1)} %cand.1) | copy-start | bytes 393220
  1.4 3.3 %copy-start.3 = (s32[2048]{0:T(1024)S(1)}, s32[2048]{0:T(1024)}, u32[]{:S(2)}) copy-start(s32[2048]{0:T(1024)} %param.16) | copy-start | bytes 24580
  1.5 3.3 %copy-start.4 = (s32[8,8]{1,0:T(8,128)S(1)}, s32[8,8]{1,0:T(8,128)}, u32[]{:S(2)}) copy-start(s32[8,8]{1,0:T(8,128)} %vis.1) | copy-start | bytes 772
  4.8 1.6 %copy-start = (bf16[2,2048,256]{2,1,0:T(8,128)(2,1)S(1)}, bf16[2,2048,256]{2,1,0:T(8,128)(2,1)}, u32[]{:S(2)}) copy-start(bf16[2,2048,256]{2,1,0:T(8,128)(2,1)} %key_hbm.1) | copy-start | bytes 6291460

commit v2 on v1

--- a/solution.py
+++ b/solution.py
@@ -12,7 +12,7 @@
 LANES = 128
 PER = LANES // DH
 GROUP_ROWS = 256
-KEY_CHUNK = 512
+KEY_CHUNK = 1024
 BIG = 16384.0
 MESH = pl.DeviceIdType.MESH
 
@@ -29,6 +29,7 @@
 
 def kernel(
     n,
+    inner,
     cand,
     w_in,
     key_hbm,
@@ -49,6 +50,8 @@
     qaug,
     part,
     parts_in,
+    pair_in,
+    merged,
     acc,
     att_send,
     att_in,
@@ -59,6 +62,9 @@
     q_recv,
     p_send,
     p_recv,
+    f_send,
+    y_send,
+    y_recv,
     h_send,
     h_recv,
 ):
@@ -75,6 +81,10 @@
     group_rows = min(GROUP_ROWS, total)
     per_group = group_rows // rows
     groups = n // per_group
+    outer = n // inner
+    relay = inner == 2 and per_group == inner
+    line, side = me // inner, lax.rem(me, inner)
+    beside = line * inner + (inner - 1 - side)
     key_chunk = min(KEY_CHUNK, hist_dev)
 
     load_k = pltpu.make_async_copy(key_hbm, keys, load_sem.at[0])
@@ -121,6 +131,43 @@
             device_id={"hist": s},
             device_id_type=MESH,
         )
+
+    def f_copy(l, z, owner):
+        return pltpu.make_async_remote_copy(
+            src_ref=qall.at[l, row_of(owner)],
+            dst_ref=qall.at[l, row_of(owner)],
+            send_sem=f_send.at[l, z],
+            recv_sem=q_recv.at[l, owner],
+            device_id={"hist": beside},
+            device_id_type=MESH,
+        )
+
+    def y_copy(l, z):
+        return pltpu.make_async_remote_copy(
+            src_ref=part.at[l, row_of(z * inner + (inner - 1 - side))],
+            dst_ref=pair_in.at[l, z],
+            send_sem=y_send.at[l, z],
+            recv_sem=y_recv.at[l, z],
+            device_id={"hist": beside},
+            device_id_type=MESH,
+        )
+
+    def m_copy(l, z, owner):
+        return pltpu.make_async_remote_copy(
+            src_ref=merged.at[l, z],
+            dst_ref=parts_in.at[l, owner],
+            send_sem=p_send.at[l, z],
+            recv_sem=p_recv.at[l, owner],
+            device_id={"hist": z * inner + side},
+            device_id_type=MESH,
+        )
+
+    def merge(l, z):
+        y_copy(l, z).wait_recv()
+        both = part[l, row_of(z * inner + side), :].astype(jnp.float32)
+        both = both + pair_in[l, z].astype(jnp.float32)
+        merged[l, z] = both.astype(jnp.bfloat16)
+        m_copy(l, z, line).start()
 
     def build_keys():
         lane = lax.broadcasted_iota(jnp.int32, (LANES, LANES), 1)
@@ -187,7 +234,7 @@
     row_q = lax.broadcasted_iota(jnp.int32, (group_rows, LANES), 0)
     lane_a = lax.broadcasted_iota(jnp.int32, (group_rows, LANES), 1)
 
-    def attend(l, g):
+    def attend(l, g, between):
         span = pl.ds(pl.multiple_of(g * group_rows, group_rows), group_rows)
         which = (row_q + g * group_rows) // micro_rows
         for h in range(heads):
@@ -217,7 +264,10 @@
                 acc[:, p * LANES : (p + 1) * LANES] += jnp.where(lane_a < DH, found[0], found[1])
             return carry
 
-        lax.fori_loop(0, hist_dev // key_chunk, chunk, 0)
+        steps = hist_dev // key_chunk
+        lax.fori_loop(0, steps // 2, chunk, 0)
+        between()
+        lax.fori_loop(steps // 2, steps, chunk, 0)
         part[l, span, :] = acc[...].astype(jnp.bfloat16)
 
     block_row = lax.broadcasted_iota(jnp.int32, (wl, wl), 0) // DH
@@ -238,8 +288,13 @@
         qall[l, row_of(me), :] = (queries * (0.5 * DH**-0.5)).astype(jnp.bfloat16)
         if l == 0:
             pl.semaphore_wait(barrier, n)
-        for j in range(1, n):
-            q_copy(l, lax.rem(me + j, n), me).start()
+        if relay:
+            q_copy(l, beside, me).start()
+            for j in range(1, outer):
+                q_copy(l, lax.rem(line + outer - j, outer) * inner + side, me).start()
+        else:
+            for j in range(1, n):
+                q_copy(l, lax.rem(me + j, n), me).start()
         keys_new = project(1).astype(jnp.float32)
         values_new = project(2).astype(jnp.float32)
         gates = project(3)
@@ -267,7 +322,7 @@
                 def _():
                     q_copy(l, s, s).wait_recv()
 
-            attend(l, g)
+            attend(l, g, lambda: None)
             for i in range(per_group):
                 s = g * per_group + i
 
@@ -277,12 +332,44 @@
 
             return carry
 
-        lax.fori_loop(0, groups, group, 0)
-        history = part[l, row_of(me), :].astype(jnp.float32)
-        for j in range(1, n):
-            s = lax.rem(me + j, n)
-            p_copy(l, s, s).wait_recv()
-            history = history + parts_in[l, s].astype(jnp.float32)
+        def relayed(t, carry):
+            z = lax.rem(line + t, outer)
+            after = lax.rem(line + t + 1, outer)
+            before = lax.rem(line + t + outer - 1, outer)
+            q_copy(l, z * inner + (inner - 1 - side), z * inner + (inner - 1 - side)).wait_recv()
+
+            def between():
+                @pl.when(t < outer - 1)
+                def _():
+                    q_copy(l, after * inner + side, after * inner + side).wait_recv()
+                    f_copy(l, after, after * inner + side).start()
+
+                @pl.when(t > 1)
+                def _():
+                    merge(l, before)
+
+            attend(l, z, between)
+            y_copy(l, z).start()
+            return carry
+
+        if relay:
+            lax.fori_loop(0, outer, relayed, 0)
+            if outer > 1:
+                merge(l, lax.rem(line + outer - 1, outer))
+            y_copy(l, line).wait_recv()
+            history = part[l, row_of(me), :].astype(jnp.float32)
+            history = history + pair_in[l, line].astype(jnp.float32)
+            for j in range(1, outer):
+                z = lax.rem(line + outer - j, outer)
+                m_copy(l, z, z).wait_recv()
+                history = history + parts_in[l, z].astype(jnp.float32)
+        else:
+            lax.fori_loop(0, groups, group, 0)
+            history = part[l, row_of(me), :].astype(jnp.float32)
+            for j in range(1, n):
+                s = lax.rem(me + j, n)
+                p_copy(l, s, s).wait_recv()
+                history = history + parts_in[l, s].astype(jnp.float32)
         attended = history + own
         att_send[l] = attended
         att_copy = to_head(att_send.at[l], att_in.at[l], 2 * l + 1)
@@ -310,15 +397,25 @@
         att_copy.wait_send()
         if l == 0:
             w_copy.wait_send()
-        for j in range(1, n):
-            s = lax.rem(me + j, n)
-            q_copy(l, s, me).wait_send()
-            p_copy(l, s, me).wait_send()
+        if relay:
+            q_copy(l, beside, me).wait_send()
+            y_copy(l, line).wait_send()
+            for j in range(1, outer):
+                z = lax.rem(line + j, outer)
+                q_copy(l, z * inner + side, me).wait_send()
+                f_copy(l, z, z * inner + side).wait_send()
+                y_copy(l, z).wait_send()
+                m_copy(l, z, line).wait_send()
+        else:
+            for j in range(1, n):
+                s = lax.rem(me + j, n)
+                q_copy(l, s, me).wait_send()
+                p_copy(l, s, me).wait_send()
     out[...] = stream.astype(out.dtype)
 
 
 def shards(
-    n, candidates, key_cache, value_cache, w_in, w_out, rab_table, hist_len, hist_bucket, visible
+    n, inner, candidates, key_cache, value_cache, w_in, w_out, rab_table, hist_len, hist_bucket, visible
 ):
     layers, hist_dev, wl = key_cache.shape
     rows, d = candidates.shape
@@ -331,7 +428,7 @@
     hbm = pl.BlockSpec(memory_space=pl.ANY)
     dma = pltpu.SemaphoreType.DMA
     return pl.pallas_call(
-        functools.partial(kernel, n),
+        functools.partial(kernel, n, inner),
         out_shape=jax.ShapeDtypeStruct((rows, d), bf16),
         in_specs=[vmem, vmem, hbm, hbm, vmem, vmem, vmem, smem, smem],
         out_specs=vmem,
@@ -346,12 +443,17 @@
             pltpu.VMEM((heads, group_rows, LANES), bf16),
             pltpu.VMEM((layers, total, wl), bf16),
             pltpu.VMEM((layers, n, rows, wl), bf16),
+            pltpu.VMEM((layers, n // inner, rows, wl), bf16),
+            pltpu.VMEM((layers, n // inner, rows, wl), bf16),
             pltpu.VMEM((group_rows, wl), f32),
             pltpu.VMEM((layers, rows, wl), f32),
             pltpu.VMEM((layers, rows, wl), f32),
             pltpu.VMEM((layers, rows, wl), bf16),
             pltpu.VMEM((layers, rows, wl), bf16),
             dma((2,)),
+            dma((layers, n)),
+            dma((layers, n)),
+            dma((layers, n)),
             dma((layers, n)),
             dma((layers, n)),
             dma((layers, n)),
@@ -375,6 +477,18 @@
     )
 
 
+def inner_of(mesh):
+    n = mesh.shape["hist"]
+    if n % 2 or n < 4:
+        return 1
+    index = [slice(None) if name == "hist" else 0 for name in mesh.axis_names]
+    spots = [getattr(device, "coords", None) for device in mesh.devices[tuple(index)][:3]]
+    if any(spot is None for spot in spots):
+        return 1
+    apart = [sum(abs(a - b) for a, b in zip(spots[0], spot)) for spot in spots[1:]]
+    return 2 if apart == [1, 1] else 1
+
+
 def solution(mesh):
     placed = (
         P(("users", "hist"), None),
@@ -388,7 +502,7 @@
         P(None, ("users", "hist")),
     )
     return jax.shard_map(
-        functools.partial(shards, mesh.shape["hist"]),
+        functools.partial(shards, mesh.shape["hist"], inner_of(mesh)),
         mesh=mesh,
         in_specs=placed,
         out_specs=P(("users", "hist"), None),

time: 78 us -> 71.9 us (0.922)
  Pallas kernels: 70.7 us -> 64.6 us
    pallas_call x1, Pallas kernels: 70.7 us -> 64.6 us  [shards(): pl.pallas_call(functools.partial(kernel, n, inner), out_shape=jax.ShapeDt...]
where the time goes in v2:
time: 71.9 us; the launch traced here: 71.7 us
  Pallas kernels  64.6 us (90%)
  local copies, waits for them, and re-layouts  6.34 us (9%)
  between operations  0.73 us (1%)
    pallas_call x1, Pallas kernels, shards(): pl.pallas_call(functools.partial(kernel, n, inner), out_shape=jax.ShapeDt...  64.6 us
    reshape x1, local copies, waits for them, and re-layouts, shards(): w_in.reshape(layers, d, 4 * wl)  3.29 us
    unnamed x12, local copies, waits for them, and re-layouts  3.04 us

profile of v2, /device:TPU:1, one launch (start us, length us, event | category | flops | bytes accessed | tf_op | source)
XLA Modules:
  0.0 71.7 jit_solution(6351255995360603597)
XLA Ops:
  0.7 0.8 %copy.10.rab = f32[2,32,4]{2,1,0:T(8,128)S(1)} copy(f32[2,32,4]{1,2,0:T(4,128)} %param.14) | data formatting | bytes 2048 | tf_op args[5]
  1.4 0.0 copy-start.1
  1.4 0.0 copy-start.2
  1.4 0.0 copy-start.3
  1.5 0.0 copy-start.4
  1.5 3.3 %reshape.6.w_in = bf16[2,512,1024]{2,1,0:T(8,128)(2,1)S(1)} reshape(bf16[2,512,4,256]{3,2,1,0:T(4,128)(2,1)} %param.12) | data formatting | bytes 4194304 | tf_op jit(solution)/shard_map/reshape | solution.py:469
  4.8 0.0 copy-done.1
  4.8 0.0 copy-done.2
  4.8 0.0 copy-done.3
  4.8 0.0 copy-done.4
  4.8 0.0 copy-start
  4.8 1.6 %copy-done = bf16[2,2048,256]{2,1,0:T(8,128)(2,1)S(1)} copy-done((bf16[2,2048,256]{2,1,0:T(8,128)(2,1)S(1)}, bf16[2,2048,256]{2,1,0:T(8,128)(2,1)}, u32[]{:S(2)}) %copy-start) | copy-done | bytes 2097176
  6.4 64.6 %shard_map.91 = bf16[128,512]{1,0:T(8,128)(2,1)S(1)} custom-call(bf16[128,512]{1,0:T(8,128)(2,1)S(1)} %copy-done.2, bf16[2,512,1024]{2,1,0:T(8,128)(2,1)S(1)} %reshape.6.w_in, bf16[2,2048,256]{2,1,0:T(8,128)(2,1)S(1)} %copy-done, bf16[2,2048,256]{2,1,0:T(8,128)(2,1)} %val_hbm.1, bf16[2,256,512]{2,1,0:T(8,128)(2,1)S(1)} %copy-done.1, ...), custom_call_target="tpu_custom_call" | custom-call | tf_op jit(solution)/shard_map/pallas_call | solution.py:430
  71.0 0.7 copy.13
Async XLA Ops:
  1.4 3.3 %copy-start.1 = (bf16[2,256,512]{2,1,0:T(8,128)(2,1)S(1)}, bf16[2,256,512]{2,1,0:T(8,128)(2,1)}, u32[]{:S(2)}) copy-start(bf16[2,256,512]{2,1,0:T(8,128)(2,1)} %w_out.1) | copy-start | bytes 1572868
  1.4 3.4 %copy-start.2 = (bf16[128,512]{1,0:T(8,128)(2,1)S(1)}, bf16[128,512]{1,0:T(8,128)(2,1)}, u32[]{:S(2)}) copy-start(bf16[128,512]{1,0:T(8,128)(2,1)} %cand.1) | copy-start | bytes 393220
  1.4 3.3 %copy-start.3 = (s32[2048]{0:T(1024)S(1)}, s32[2048]{0:T(1024)}, u32[]{:S(2)}) copy-start(s32[2048]{0:T(1024)} %param.16) | copy-start | bytes 24580
  1.5 3.3 %copy-start.4 = (s32[8,8]{1,0:T(8,128)S(1)}, s32[8,8]{1,0:T(8,128)}, u32[]{:S(2)}) copy-start(s32[8,8]{1,0:T(8,128)} %vis.1) | copy-start | bytes 772
  4.8 1.6 %copy-start = (bf16[2,2048,256]{2,1,0:T(8,128)(2,1)S(1)}, bf16[2,2048,256]{2,1,0:T(8,128)(2,1)}, u32[]{:S(2)}) copy-start(bf16[2,2048,256]{2,1,0:T(8,128)(2,1)} %key_hbm.1) | copy-start | bytes 6291460

commit v3 on v2

--- a/solution.py
+++ b/solution.py
@@ -12,7 +12,7 @@
 LANES = 128
 PER = LANES // DH
 GROUP_ROWS = 256
-KEY_CHUNK = 1024
+KEY_CHUNK = 2048
 BIG = 16384.0
 MESH = pl.DeviceIdType.MESH
 
@@ -62,7 +62,6 @@
     q_recv,
     p_send,
     p_recv,
-    f_send,
     y_send,
     y_recv,
     h_send,
@@ -129,16 +128,6 @@
             send_sem=p_send.at[l, s],
             recv_sem=p_recv.at[l, owner],
             device_id={"hist": s},
-            device_id_type=MESH,
-        )
-
-    def f_copy(l, z, owner):
-        return pltpu.make_async_remote_copy(
-            src_ref=qall.at[l, row_of(owner)],
-            dst_ref=qall.at[l, row_of(owner)],
-            send_sem=f_send.at[l, z],
-            recv_sem=q_recv.at[l, owner],
-            device_id={"hist": beside},
             device_id_type=MESH,
         )
 
@@ -234,7 +223,7 @@
     row_q = lax.broadcasted_iota(jnp.int32, (group_rows, LANES), 0)
     lane_a = lax.broadcasted_iota(jnp.int32, (group_rows, LANES), 1)
 
-    def attend(l, g, between):
+    def attend(l, g):
         span = pl.ds(pl.multiple_of(g * group_rows, group_rows), group_rows)
         which = (row_q + g * group_rows) // micro_rows
         for h in range(heads):
@@ -264,10 +253,7 @@
                 acc[:, p * LANES : (p + 1) * LANES] += jnp.where(lane_a < DH, found[0], found[1])
             return carry
 
-        steps = hist_dev // key_chunk
-        lax.fori_loop(0, steps // 2, chunk, 0)
-        between()
-        lax.fori_loop(steps // 2, steps, chunk, 0)
+        lax.fori_loop(0, hist_dev // key_chunk, chunk, 0)
         part[l, span, :] = acc[...].astype(jnp.bfloat16)
 
     block_row = lax.broadcasted_iota(jnp.int32, (wl, wl), 0) // DH
@@ -289,9 +275,11 @@
         if l == 0:
             pl.semaphore_wait(barrier, n)
         if relay:
+            for j in range(1, outer):
+                z = lax.rem(line + outer - j, outer)
+                q_copy(l, z * inner + side, me).start()
+                q_copy(l, z * inner + (inner - 1 - side), me).start()
             q_copy(l, beside, me).start()
-            for j in range(1, outer):
-                q_copy(l, lax.rem(line + outer - j, outer) * inner + side, me).start()
         else:
             for j in range(1, n):
                 q_copy(l, lax.rem(me + j, n), me).start()
@@ -322,7 +310,7 @@
                 def _():
                     q_copy(l, s, s).wait_recv()
 
-            attend(l, g, lambda: None)
+            attend(l, g)
             for i in range(per_group):
                 s = g * per_group + i
 
@@ -333,29 +321,25 @@
             return carry
 
         def relayed(t, carry):
-            z = lax.rem(line + t, outer)
-            after = lax.rem(line + t + 1, outer)
-            before = lax.rem(line + t + outer - 1, outer)
-            q_copy(l, z * inner + (inner - 1 - side), z * inner + (inner - 1 - side)).wait_recv()
-
-            def between():
-                @pl.when(t < outer - 1)
+            z = lax.rem(line + t + 1, outer)
+            for i in range(inner):
+                s = z * inner + i
+
+                @pl.when(s != me)
                 def _():
-                    q_copy(l, after * inner + side, after * inner + side).wait_recv()
-                    f_copy(l, after, after * inner + side).start()
-
-                @pl.when(t > 1)
-                def _():
-                    merge(l, before)
-
-            attend(l, z, between)
+                    q_copy(l, s, s).wait_recv()
+
+            attend(l, z)
             y_copy(l, z).start()
+
+            @pl.when(t > 0)
+            def _():
+                merge(l, lax.rem(line + t, outer))
+
             return carry
 
         if relay:
             lax.fori_loop(0, outer, relayed, 0)
-            if outer > 1:
-                merge(l, lax.rem(line + outer - 1, outer))
             y_copy(l, line).wait_recv()
             history = part[l, row_of(me), :].astype(jnp.float32)
             history = history + pair_in[l, line].astype(jnp.float32)
@@ -398,12 +382,11 @@
         if l == 0:
             w_copy.wait_send()
         if relay:
-            q_copy(l, beside, me).wait_send()
+            for j in range(1, n):
+                q_copy(l, lax.rem(me + j, n), me).wait_send()
             y_copy(l, line).wait_send()
             for j in range(1, outer):
                 z = lax.rem(line + j, outer)
-                q_copy(l, z * inner + side, me).wait_send()
-                f_copy(l, z, z * inner + side).wait_send()
                 y_copy(l, z).wait_send()
                 m_copy(l, z, line).wait_send()
         else:
@@ -457,7 +440,6 @@
             dma((layers, n)),
             dma((layers, n)),
             dma((layers, n)),
-            dma((layers, n)),
             dma((2 * layers + 1,)),
             dma((2 * layers + 1,)),
         ],

time: 71.9 us -> 66.7 us (0.928)
  Pallas kernels: 64.6 us -> 59.4 us
    pallas_call x1, Pallas kernels: 64.6 us -> 59.4 us  [shards(): pl.pallas_call(functools.partial(kernel, n, inner), out_shape=jax.ShapeDt...]
where the time goes in v3:
time: 66.7 us; the launch traced here: 66.5 us
  Pallas kernels  59.4 us (89%)
  local copies, waits for them, and re-layouts  6.34 us (10%)
  between operations  0.73 us (1%)
    pallas_call x1, Pallas kernels, shards(): pl.pallas_call(functools.partial(kernel, n, inner), out_shape=jax.ShapeDt...  59.4 us
    reshape x1, local copies, waits for them, and re-layouts, shards(): w_in.reshape(layers, d, 4 * wl)  3.29 us
    unnamed x12, local copies, waits for them, and re-layouts  3.04 us

profile of v3, /device:TPU:1, one launch (start us, length us, event | category | flops | bytes accessed | tf_op | source)
XLA Modules:
  0.0 66.5 jit_solution(372809066576771863)
XLA Ops:
  0.7 0.8 %copy.10.rab = f32[2,32,4]{2,1,0:T(8,128)S(1)} copy(f32[2,32,4]{1,2,0:T(4,128)} %param.14) | data formatting | bytes 2048 | tf_op args[5]
  1.4 0.0 copy-start.1
  1.4 0.0 copy-start.2
  1.4 0.0 copy-start.3
  1.5 0.0 copy-start.4
  1.5 3.3 %reshape.6.w_in = bf16[2,512,1024]{2,1,0:T(8,128)(2,1)S(1)} reshape(bf16[2,512,4,256]{3,2,1,0:T(4,128)(2,1)} %param.12) | data formatting | bytes 4194304 | tf_op jit(solution)/shard_map/reshape | solution.py:451
  4.8 0.0 copy-done.1
  4.8 0.0 copy-done.2
  4.8 0.0 copy-done.3
  4.8 0.0 copy-done.4
  4.8 0.0 copy-start
  4.8 1.6 %copy-done = bf16[2,2048,256]{2,1,0:T(8,128)(2,1)S(1)} copy-done((bf16[2,2048,256]{2,1,0:T(8,128)(2,1)S(1)}, bf16[2,2048,256]{2,1,0:T(8,128)(2,1)}, u32[]{:S(2)}) %copy-start) | copy-done | bytes 2097176
  6.4 59.4 %shard_map.91 = bf16[128,512]{1,0:T(8,128)(2,1)S(1)} custom-call(bf16[128,512]{1,0:T(8,128)(2,1)S(1)} %copy-done.2, bf16[2,512,1024]{2,1,0:T(8,128)(2,1)S(1)} %reshape.6.w_in, bf16[2,2048,256]{2,1,0:T(8,128)(2,1)S(1)} %copy-done, bf16[2,2048,256]{2,1,0:T(8,128)(2,1)} %val_hbm.1, bf16[2,256,512]{2,1,0:T(8,128)(2,1)S(1)} %copy-done.1, ...), custom_call_target="tpu_custom_call" | custom-call | tf_op jit(solution)/shard_map/pallas_call | solution.py:413
  65.8 0.7 copy.13
Async XLA Ops:
  1.4 3.3 %copy-start.1 = (bf16[2,256,512]{2,1,0:T(8,128)(2,1)S(1)}, bf16[2,256,512]{2,1,0:T(8,128)(2,1)}, u32[]{:S(2)}) copy-start(bf16[2,256,512]{2,1,0:T(8,128)(2,1)} %w_out.1) | copy-start | bytes 1572868
  1.4 3.4 %copy-start.2 = (bf16[128,512]{1,0:T(8,128)(2,1)S(1)}, bf16[128,512]{1,0:T(8,128)(2,1)}, u32[]{:S(2)}) copy-start(bf16[128,512]{1,0:T(8,128)(2,1)} %cand.1) | copy-start | bytes 393220
  1.4 3.3 %copy-start.3 = (s32[2048]{0:T(1024)S(1)}, s32[2048]{0:T(1024)}, u32[]{:S(2)}) copy-start(s32[2048]{0:T(1024)} %param.16) | copy-start | bytes 24580
  1.5 3.3 %copy-start.4 = (s32[8,8]{1,0:T(8,128)S(1)}, s32[8,8]{1,0:T(8,128)}, u32[]{:S(2)}) copy-start(s32[8,8]{1,0:T(8,128)} %vis.1) | copy-start | bytes 772
  4.8 1.6 %copy-start = (bf16[2,2048,256]{2,1,0:T(8,128)(2,1)S(1)}, bf16[2,2048,256]{2,1,0:T(8,128)(2,1)}, u32[]{:S(2)}) copy-start(bf16[2,2048,256]{2,1,0:T(8,128)(2,1)} %key_hbm.1) | copy-start | bytes 6291460

commit v4 on v3

--- a/solution.py
+++ b/solution.py
@@ -408,7 +408,7 @@
     bf16, f32 = jnp.bfloat16, jnp.float32
     vmem = pl.BlockSpec(memory_space=pltpu.VMEM)
     smem = pl.BlockSpec(memory_space=pltpu.SMEM)
-    hbm = pl.BlockSpec(memory_space=pl.ANY)
+    hbm = pl.BlockSpec(memory_space=pltpu.HBM)
     dma = pltpu.SemaphoreType.DMA
     return pl.pallas_call(
         functools.partial(kernel, n, inner),

time: 66.7 us -> 66.7 us (level)
  no operation moved by 1% of the time
where the time goes in v4:
time: 66.7 us; the launch traced here: 66.5 us
  Pallas kernels  59.4 us (89%)
  local copies, waits for them, and re-layouts  6.34 us (10%)
  between operations  0.73 us (1%)
    pallas_call x1, Pallas kernels, shards(): pl.pallas_call(functools.partial(kernel, n, inner), out_shape=jax.ShapeDt...  59.4 us
    reshape x1, local copies, waits for them, and re-layouts, shards(): w_in.reshape(layers, d, 4 * wl)  3.29 us
    unnamed x12, local copies, waits for them, and re-layouts  3.04 us

profile of v4, /device:TPU:1, one launch (start us, length us, event | category | flops | bytes accessed | tf_op | source)
XLA Modules:
  0.0 66.5 jit_solution(372809066576771863)
XLA Ops:
  0.7 0.8 %copy.10.rab = f32[2,32,4]{2,1,0:T(8,128)S(1)} copy(f32[2,32,4]{1,2,0:T(4,128)} %param.14) | data formatting | bytes 2048 | tf_op args[5]
  1.4 0.0 copy-start.1
  1.4 0.0 copy-start.2
  1.4 0.0 copy-start.3
  1.5 0.0 copy-start.4
  1.5 3.3 %reshape.6.w_in = bf16[2,512,1024]{2,1,0:T(8,128)(2,1)S(1)} reshape(bf16[2,512,4,256]{3,2,1,0:T(4,128)(2,1)} %param.12) | data formatting | bytes 4194304 | tf_op jit(solution)/shard_map/reshape | solution.py:451
  4.8 0.0 copy-done.1
  4.8 0.0 copy-done.2
  4.8 0.0 copy-done.3
  4.8 0.0 copy-done.4
  4.8 0.0 copy-start
  4.8 1.6 %copy-done = bf16[2,2048,256]{2,1,0:T(8,128)(2,1)S(1)} copy-done((bf16[2,2048,256]{2,1,0:T(8,128)(2,1)S(1)}, bf16[2,2048,256]{2,1,0:T(8,128)(2,1)}, u32[]{:S(2)}) %copy-start) | copy-done | bytes 2097176
  6.4 59.4 %shard_map.91 = bf16[128,512]{1,0:T(8,128)(2,1)S(1)} custom-call(bf16[128,512]{1,0:T(8,128)(2,1)S(1)} %copy-done.2, bf16[2,512,1024]{2,1,0:T(8,128)(2,1)S(1)} %reshape.6.w_in, bf16[2,2048,256]{2,1,0:T(8,128)(2,1)S(1)} %copy-done, bf16[2,2048,256]{2,1,0:T(8,128)(2,1)} %val_hbm.1, bf16[2,256,512]{2,1,0:T(8,128)(2,1)S(1)} %copy-done.1, ...), custom_call_target="tpu_custom_call" | custom-call | tf_op jit(solution)/shard_map/pallas_call | solution.py:413
  65.8 0.7 copy.13
Async XLA Ops:
  1.4 3.3 %copy-start.1 = (bf16[2,256,512]{2,1,0:T(8,128)(2,1)S(1)}, bf16[2,256,512]{2,1,0:T(8,128)(2,1)}, u32[]{:S(2)}) copy-start(bf16[2,256,512]{2,1,0:T(8,128)(2,1)} %w_out.1) | copy-start | bytes 1572868
  1.4 3.4 %copy-start.2 = (bf16[128,512]{1,0:T(8,128)(2,1)S(1)}, bf16[128,512]{1,0:T(8,128)(2,1)}, u32[]{:S(2)}) copy-start(bf16[128,512]{1,0:T(8,128)(2,1)} %cand.1) | copy-start | bytes 393220
  1.4 3.3 %copy-start.3 = (s32[2048]{0:T(1024)S(1)}, s32[2048]{0:T(1024)}, u32[]{:S(2)}) copy-start(s32[2048]{0:T(1024)} %param.16) | copy-start | bytes 24580
  1.5 3.3 %copy-start.4 = (s32[8,8]{1,0:T(8,128)S(1)}, s32[8,8]{1,0:T(8,128)}, u32[]{:S(2)}) copy-start(s32[8,8]{1,0:T(8,128)} %vis.1) | copy-start | bytes 772
  4.8 1.6 %copy-start = (bf16[2,2048,256]{2,1,0:T(8,128)(2,1)S(1)}, bf16[2,2048,256]{2,1,0:T(8,128)(2,1)}, u32[]{:S(2)}) copy-start(bf16[2,2048,256]{2,1,0:T(8,128)(2,1)} %key_hbm.1) | copy-start | bytes 6291460
